TPU v7x, 256 devices: a whole 4x4x8 slice. The times are simulated.
256 devices in a mesh: leaf: 2 (over core), row: 16 (over z, x_lo), col: 8 (over y, x_hi).
Axes of the slice: x: 4 (x_hi: 2, x_lo: 2; x = x_hi * 2 + x_lo), y: 4, z: 8, core: 2. Of those that a mesh axis runs over, the one named last changes fastest.
Arguments:
- child_tiles: float32 [1024, 64, 4096], P(('leaf', 'row'), None, 'col'), may hold values from -0.078125 to 0.078125
- block_mask: int32 [1024, 64], P(('leaf', 'row'), 'col'), may hold values 0 or 1
- destination: int32 [1024, 1], P(('leaf', 'row')), may hold values from 0 to 31; in each aligned block of 32 rows (0 to 31, 32 to 63, ...) at most 2 rows name the same one
Outputs:
- r_top: float32 [2, 128, 4096], P('leaf', None, 'col')
Inputs may be any that keep to these rules, and one draw needn't show every extreme that they name: Among the tiles of one device, no destination is named more than 2 times, a bound that some block reaches.
All inputs are finite; a program needn't handle non-finite values. No bound on the sum of `block_mask` on one device may be relied on, other than what follows from the above.
Results may differ from a plain program's by a relative error of at most 0.0003.
Values sent between devices are 32-bit elements; how exact they have to be, the bound alone decides.
A program may use at most 64 MiB of HBM per device.

v0:
```python
import jax
import jax.numpy as jnp
from jax import lax
from jax.sharding import PartitionSpec as P

PANELS = 2
CAP = 2


def spread(shard, axis, root):
    mine = lax.axis_index(axis) == root
    return lax.psum(jnp.where(mine, shard, jnp.zeros_like(shard)), axis)


def per_device(child_tiles, block_mask, destination):
    tile_count, block_size, columns_dev = child_tiles.shape
    blocks_dev = columns_dev // block_size
    leaf_count = lax.axis_size("leaf")
    row_count = lax.axis_size("row")
    col_count = lax.axis_size("col")
    targets_all = leaf_count * row_count
    slot_count = targets_all * CAP
    masked_tiles = child_tiles.reshape(tile_count, block_size, blocks_dev, block_size)
    masked_tiles = masked_tiles * block_mask.astype(jnp.float32)[:, None, :, None]
    target_dev = destination[:, 0]
    target_hits = (target_dev[:, None] == jnp.arange(targets_all, dtype=jnp.int32)[None, :]).astype(
        jnp.int32
    )
    earlier = jnp.cumsum(target_hits, axis=0) - target_hits
    rank_in = jnp.sum(target_hits * earlier, axis=1)
    slot_index = target_dev * CAP + rank_in
    placing = (slot_index[None, :] == jnp.arange(slot_count, dtype=jnp.int32)[:, None]).astype(
        jnp.float32
    )
    packed = jnp.dot(
        placing,
        masked_tiles.reshape(tile_count, block_size * columns_dev),
        precision=lax.Precision.HIGHEST,
    )
    arrived = lax.all_to_all(
        packed.reshape(targets_all, CAP, block_size, columns_dev),
        ("leaf", "row"),
        split_axis=0,
        concat_axis=0,
        tiled=True,
    )
    front_rows = arrived.reshape(slot_count * block_size, columns_dev)
    col_place = lax.axis_index("col")
    eliminated_index = jnp.repeat(
        jnp.arange(blocks_dev, dtype=jnp.int32) * col_count + col_place, block_size
    )
    output_rows = []
    for panel_update in range(PANELS):
        owner_col = panel_update % col_count
        local_block = panel_update // col_count
        panel_cols = front_rows[:, local_block * block_size : (local_block + 1) * block_size]
        panel_cols = spread(panel_cols, "col", owner_col)
        gram_part = jnp.dot(panel_cols.T, panel_cols, precision=lax.Precision.HIGHEST)
        cross_part = jnp.dot(panel_cols.T, front_rows, precision=lax.Precision.HIGHEST)
        gram_sum, cross_sum = lax.psum((gram_part, cross_part), "row")
        lower_factor = jnp.linalg.cholesky(gram_sum)
        reflector_coefficients = lax.linalg.triangular_solve(
            lower_factor, cross_sum, left_side=True, lower=True
        )
        output_rows.append(
            jnp.where((eliminated_index >= panel_update)[None, :], reflector_coefficients, 0.0)
        )
        basis_cols = lax.linalg.triangular_solve(
            lower_factor, panel_cols, left_side=False, lower=True, transpose_a=True
        )
        trailing_part = jnp.where(
            (eliminated_index > panel_update)[None, :], reflector_coefficients, 0.0
        )
        front_rows = front_rows - jnp.dot(
            basis_cols, trailing_part, precision=lax.Precision.HIGHEST
        )
    return jnp.concatenate(output_rows, axis=0)[None]


def solution(mesh):
    in_specs = (
        P(("leaf", "row"), None, "col"),
        P(("leaf", "row"), "col"),
        P(("leaf", "row"), None),
    )
    out_specs = P("leaf", None, "col")
    return jax.shard_map(
        per_device, mesh=mesh, in_specs=in_specs, out_specs=out_specs, check_vma=False
    )
```

profile of v0, /device:TPU:2, one launch (start us, length us, event | category | flops | bytes accessed | tf_op | source)
XLA Modules:
  0.0 901.4 jit_solution(17468077856885979438)
XLA Ops:
  9.6 3.8 mul.31
  13.4 6.9 mul.32
  20.3 4.8 copy.31
  25.5 3.6 fusion
  29.2 8.1 copy.20
  37.2 10.1 %all-to-all-start = ((f32[32,2,64,512]{3,2,1,0:T(8,128)}), f32[32,2,64,512]{3,2,1,0:T(8,128)}, u32[]{:S(2)}, u32[]{:S(2)}) async-start(f32[32,2,64,512]{3,2,1,0:T(8,128)} %copy.20), calls=%async_computation | async-start | bytes 16777216 | tf_op jit(solution)/shard_map/all_to_all | solution.py:40
  47.4 185.3 %all-to-all-done = f32[32,2,64,512]{3,2,1,0:T(8,128)} async-done(((f32[32,2,64,512]{3,2,1,0:T(8,128)}), f32[32,2,64,512]{3,2,1,0:T(8,128)}, u32[]{:S(2)}, u32[]{:S(2)}) %all-to-all-start) | async-done | bytes 8388640 | tf_op jit(solution)/shard_map/all_to_all | solution.py:40
  232.7 8.9 copy.21
  244.4 98.5 %all-reduce.5.cloned.1.call-done = f32[4096,64]{0,1:T(8,128)} async-done(((f32[4096,64]{0,1:T(8,128)}), f32[4096,64]{0,1:T(8,128)}) %all-reduce.5.cloned.1.call-update) | async-done | bytes 1048592 | tf_op jit(solution)/shard_map/psum | solution.py:12
  342.9 2.6 fusion.20
  345.5 60.1 %psum.43 = f32[64,64]{0,1:T(8,128)S(1)} all-reduce(f32[64,64]{0,1:T(8,128)S(1)} %fusion.20), channel_id=1, replica_groups=mesh['leaf'=2,'row'=16,'col'=8] {'row'}, use_global_device_ids=true, to_apply=%region_3.4 | all-reduce | flops 4096 | bytes 32768 | tf_op jit(solution)/shard_map/psum | solution.py:60
  405.7 5.8 cholesky.44
  412.9 4.9 custom-call.10
  417.8 9.6 %fusion.21 = f32[64,512]{1,0:T(8,128)} fusion(f32[4096,64]{0,1:T(8,128)} %all-reduce.5.cloned.1.call-done, f32[4096,512]{1,0:T(8,128)} %bitcast.5), kind=kOutput, calls=%fused_computation.46 | convolution fusion | flops 1610612736 | bytes 9568256 | tf_op jit(solution)/shard_map/dot_general | solution.py:59
  428.5 135.3 %all-reduce.7.cloned.1.call-done = f32[64,512]{1,0:T(8,128)} async-done(((f32[64,512]{1,0:T(8,128)}), f32[64,512]{1,0:T(8,128)}) %all-reduce.7.cloned.1.call-update) | async-done | bytes 131088 | tf_op jit(solution)/shard_map/psum | solution.py:60
  565.0 9.5 %convolution_subtract_fusion = f32[4096,512]{0,1:T(8,128)S(1)} fusion(f32[4096,512]{0,1:T(8,128)} %copy.21, f32[4096,64]{0,1:T(8,128)S(1)} %fusion.9, f32[64,512]{1,0:T(8,128)S(1)} %get-tuple-element.8, pred[512]{0:T(512)(128)(4,1)S(1)} %gt.12), kind=kOutput, calls=%fused_computation | convolution fusion | flops 1612742656 | bytes 17957376 | tf_op jit(solution)/shard_map/dot_general | solution.py:74
  574.5 3.2 copy-done
  579.0 95.1 %all-reduce.9.cloned.1.call-done = f32[4096,64]{0,1:T(8,128)} async-done(((f32[4096,64]{0,1:T(8,128)}), f32[4096,64]{0,1:T(8,128)}) %all-reduce.9.cloned.1.call-update) | async-done | bytes 1048592 | tf_op jit(solution)/shard_map/psum | solution.py:12
  674.2 2.7 fusion.22
  676.9 60.4 %psum.46 = f32[64,64]{0,1:T(8,128)S(1)} all-reduce(f32[64,64]{0,1:T(8,128)S(1)} %fusion.22), channel_id=1, replica_groups=mesh['leaf'=2,'row'=16,'col'=8] {'row'}, use_global_device_ids=true, to_apply=%region_8.11 | all-reduce | flops 4096 | bytes 32768 | tf_op jit(solution)/shard_map/psum | solution.py:60
  737.4 5.8 cholesky.55
  743.9 12.4 %fusion.23 = f32[64,512]{1,0:T(8,128)} fusion(f32[4096,64]{0,1:T(8,128)} %all-reduce.9.cloned.1.call-done, f32[4096,512]{0,1:T(8,128)} %copy-done), kind=kOutput, calls=%fused_computation.48 | convolution fusion | flops 1610612736 | bytes 9568256 | tf_op jit(solution)/shard_map/dot_general | solution.py:59
  757.0 4.9 custom-call.11
  761.9 130.9 %all-reduce.11.cloned.1.call-done = f32[64,512]{1,0:T(8,128)} async-done(((f32[64,512]{1,0:T(8,128)}), f32[64,512]{1,0:T(8,128)}) %all-reduce.11.cloned.1.call-update) | async-done | bytes 131088 | tf_op jit(solution)/shard_map/psum | solution.py:60
  (45 shorter events, 14.6 us)
Async XLA Ops:
  20.3 4.8 copy-start.1
  37.2 195.5 %all-to-all-start = ((f32[32,2,64,512]{3,2,1,0:T(8,128)}), f32[32,2,64,512]{3,2,1,0:T(8,128)}, u32[]{:S(2)}, u32[]{:S(2)}) async-start(f32[32,2,64,512]{3,2,1,0:T(8,128)} %copy.20), calls=%async_computation | async-start | bytes 16777216 | tf_op jit(solution)/shard_map/all_to_all | solution.py:40
  47.4 295.5 %all-reduce.5.cloned.1.call-start = ((), (), s32[]{:S(2)}) async-start(), calls=%async_computation.1 | async-start | bytes 2097152 | tf_op jit(solution)/shard_map/psum | solution.py:12
  244.0 319.8 %all-reduce.7.cloned.1.call-start = ((), (), s32[]{:S(2)}) async-start(), calls=%async_computation.2 | async-start | bytes 262144 | tf_op jit(solution)/shard_map/psum | solution.py:60
  342.9 84.6 %copy-start.2 = (f32[4096,64]{0,1:T(8,128)S(1)}, f32[4096,64]{0,1:T(8,128)}, u32[]{:S(2)}) copy-start(f32[4096,64]{0,1:T(8,128)} %all-reduce.5.cloned.1.call-done) | copy-start | bytes 3145732
  427.4 246.8 %all-reduce.9.cloned.1.call-start = ((), (), s32[]{:S(2)}) async-start(), calls=%async_computation.3 | async-start | bytes 2097152 | tf_op jit(solution)/shard_map/psum | solution.py:12
  574.5 3.2 copy-start
  578.8 314.0 %all-reduce.11.cloned.1.call-start = ((), (), s32[]{:S(2)}) async-start(), calls=%async_computation.4 | async-start | bytes 262144 | tf_op jit(solution)/shard_map/psum | solution.py:60
Sparse Core Ops, SparseCore 0:
  244.1 98.6 all-reduce.4
  427.5 136.2 all-reduce.6
  578.9 95.1 all-reduce.8
  756.5 136.2 all-reduce.10
where the time goes:
time: 914 us; the launch traced here: 901 us
  waiting for transfers between devices  645 us (71%)
  blocking collectives  120 us (13%)
  matrix products  43.9 us (5%)
  local copies, waits for them, and re-layouts  36.4 us (4%)
  other arithmetic  31.7 us (3%)
  between operations  13.5 us (1%)
  starting transfers between devices  10.3 us (1%)
    psum x2, waiting for transfers between devices, per_device(): gram_sum, cross_sum = lax.psum((gram_part, cross_part), 'row')  266 us
    psum x2, waiting for transfers between devices, spread(): return lax.psum(jnp.where(mine, shard, jnp.zeros_like(shard)), axis)  194 us
    all_to_all x1, waiting for transfers between devices, per_device(): lax.all_to_all(packed.reshape(targets_all, CAP, block_size, columns_dev),...  185 us
    psum x2, blocking collectives, per_device(): gram_sum, cross_sum = lax.psum((gram_part, cross_part), 'row')  120 us
    dot_general x2, matrix products, per_device(): jnp.dot(panel_cols.T, front_rows, precision=lax.Precision.HIGHEST)  22 us
  transfers between devices with their start and end apart: 5, of which 5 were waited for; matrix products, arithmetic and copies ran while one was open for 1% of the time, Pallas kernels for 0%

commit v1 on v0

v1 whole, which is shorter than its diff:
```python
import jax
import jax.numpy as jnp
from jax import lax
from jax.sharding import PartitionSpec as P

FRONTS = 2


def per_device(child_tiles, block_mask, destination):
    tile_count, edge, columns_dev = child_tiles.shape
    blocks_dev = columns_dev // edge
    col = lax.axis_index("col")
    per_front = lax.axis_size("row")
    mask = block_mask.astype(jnp.float32)
    rows = tile_count * edge
    tiles = child_tiles.reshape(rows, columns_dev)
    own = tiles[:, :edge] * jnp.repeat(mask[:, 0], edge)[:, None]
    panel = jnp.concatenate([jnp.where(col == k, own, 0.0) for k in range(2)], axis=1)
    panel = lax.psum(panel, "col")
    front = jnp.repeat(destination[:, 0] // per_front, edge)[:, None]
    left = jnp.concatenate([jnp.where(front == f, panel, 0.0) for f in range(FRONTS)], axis=1)
    masked = (tiles.reshape(tile_count, edge, blocks_dev, edge) * mask[:, None, :, None]).reshape(rows, columns_dev)
    dot = lambda a, b: lax.dot_general(a, b, (((0,), (0,)), ((), ())), precision=lax.Precision.HIGHEST)
    sums = jnp.concatenate([dot(left, masked), dot(left, panel)], axis=1)
    sums = lax.psum_scatter(sums, "leaf", scatter_dimension=0, tiled=True)
    sums = lax.psum(sums, "row")
    cross, gram = sums[:, :columns_dev], sums[:, columns_dev:]
    lower = jnp.linalg.cholesky(gram)
    top = lax.linalg.triangular_solve(lower, cross, left_side=True, lower=True)
    col_count = lax.axis_size("col")
    place = jnp.repeat(jnp.arange(blocks_dev) * col_count + col, edge)
    line = jnp.arange(2 * edge) // edge
    return jnp.where(place[None, :] >= line[:, None], top, 0.0)[None]


def solution(mesh):
    in_specs = (
        P(("leaf", "row"), None, "col"),
        P(("leaf", "row"), "col"),
        P(("leaf", "row"), None),
    )
    return jax.shard_map(
        per_device, mesh=mesh, in_specs=in_specs, out_specs=P("leaf", None, "col"), check_vma=False
    )
```

time: 914 us -> 310 us (0.34)
  the two profiles are of different devices: /device:TPU:2 before, /device:TPU:6 now
where the time goes in v1:
time: 310 us; the launch traced here: 309 us
  waiting for transfers between devices  239 us (77%)
  other arithmetic  31 us (10%)
  matrix products  13.4 us (4%)
  between operations  13.2 us (4%)
  local copies, waits for them, and re-layouts  13 us (4%)
    psum x1, waiting for transfers between devices, per_device(): sums = lax.psum(sums, 'row')  140 us
    psum x1, waiting for transfers between devices, per_device(): panel = lax.psum(panel, 'col')  84 us
    reduce_scatter x1, waiting for transfers between devices, per_device(): sums = lax.psum_scatter(sums, 'leaf', scatter_dimension=0, tiled=True)  14.5 us
    another operation x3, other arithmetic, per_device(): lower = jnp.linalg.cholesky(gram)  12.4 us
    mul x2, local copies, waits for them, and re-layouts, per_device(): tiles.reshape(tile_count, edge, blocks_dev, edge) * mask[:, None, :, None]  11.3 us
    dot_general x2, matrix products, per_device(): lax.dot_general(a, b, (((0,), (0,)), ((), ())), precision=lax.Precision.H...  11.3 us
    another operation x2, other arithmetic, per_device(): top = lax.linalg.triangular_solve(lower, cross, left_side=True, lower=True)  10.5 us
  transfers between devices with their start and end apart: 3, of which 3 were waited for; matrix products, arithmetic and copies ran while one was open for 4% of the time, Pallas kernels for 0%

profile of v1, /device:TPU:6, one launch (start us, length us, event | category | flops | bytes accessed | tf_op | source)
XLA Modules:
  0.0 309.4 jit_solution(1366986369914015669)
XLA Ops:
  6.5 0.7 convert_element_type.3
  7.4 1.6 fusion.5
  9.0 1.3 pad_maximum_fusion.3
  10.5 0.1 eq.37
  10.7 0.1 eq.33
  10.8 3.8 %mul.28 = f32[32,64,8,64]{3,2,1,0:T(8,128)} broadcast(f32[32,8]{1,0:T(8,128)S(1)} %copy.4), dimensions={0,2} | broadcast | bytes 4195328 | tf_op jit(solution)/shard_map/mul | solution.py:22
  14.6 7.5 %mul.29 = f32[2048,512]{1,0:T(8,128)} reshape(f32[32,64,8,64]{3,2,1,0:T(8,128)} %mul.28) | data formatting | bytes 8388608 | tf_op jit(solution)/shard_map/mul | solution.py:22
  22.1 84.0 %all-reduce.3.cloned.1.call-done = f32[2048,128]{1,0:T(8,128)} async-done(((f32[2048,128]{1,0:T(8,128)}), f32[2048,128]{1,0:T(8,128)}) %all-reduce.3.cloned.1.call-update) | async-done | bytes 1048592 | tf_op jit(solution)/shard_map/psum | solution.py:19
  106.1 2.8 broadcast_select_fusion.1
  109.0 9.4 %fusion = f32[256,512]{0,1:T(8,128)S(1)} fusion(f32[2048,512]{1,0:T(8,128)} %bitcast.27, f32[2048,512]{1,0:T(8,128)} %mul.29, f32[2048,128]{1,0:T(8,128)S(1)} %get-tuple-element.10, f32[2048,128]{1,0:T(8,128)S(1)} %get-tuple-element.9), kind=kOutput, calls=%fused_computation | convolution fusion | flops 3222798336 | bytes 11010048 | tf_op jit(solution)/shard_map/dot_general | solution.py:23
  118.4 1.9 fusion.2
  120.3 0.9 pad_maximum_fusion.4
  121.2 0.2 all-reduce.5.cloned.1.call-start
  121.4 14.5 %reduce-scatter.2.cloned.1.call-done = f32[128,640]{0,1:T(8,128)} async-done(((f32[256,640]{0,1:T(8,128)}), f32[128,640]{0,1:T(8,128)}) %reduce-scatter.2.cloned.1.call-update) | async-done | bytes 327696 | tf_op jit(solution)/shard_map/reduce_scatter | solution.py:25
  136.1 0.1 ge.17
  136.2 140.0 %all-reduce.5.cloned.1.call-done = f32[128,640]{0,1:T(8,128)} async-done(((f32[128,640]{0,1:T(8,128)}), f32[128,640]{0,1:T(8,128)}) %all-reduce.5.cloned.1.call-update) | async-done | bytes 327696 | tf_op jit(solution)/shard_map/psum | solution.py:26
  276.1 0.8 slice.25
  277.0 0.1 copy.6
  277.1 0.9 fusion.9
  277.9 11.7 %cholesky.16 = f32[128,128]{1,0:T(8,128)S(1)} custom-call(f32[128,128]{1,0:T(8,128)S(1)} %fusion.9), custom_call_target="Cholesky" | custom-call | tf_op jit(solution)/shard_map/jit(cholesky)/cholesky | solution.py:28
  289.7 0.6 compare_reduce_fusion
  290.3 0.7 fusion.7
  291.0 9.8 %custom-call.6 = f32[1,128,128]{1,2,0:T(8,128)S(1)} custom-call(f32[1,128,128]{2,1,0:T(8,128)S(1)} %fusion.7), custom_call_target="InvertDiagBlocksLowerTriangular" | custom-call | tf_op jit(solution)/shard_map/triangular_solve | solution.py:29
  300.8 2.1 fusion.3
  (21 shorter events, 0.6 us)
Async XLA Ops:
  6.5 3.9 %copy-start.1 = (s32[32,1]{0,1:T(1,128)S(1)}, s32[32,1]{0,1:T(1,128)}, u32[]{:S(2)}) copy-start(s32[32,1]{0,1:T(1,128)} %param.5) | copy-start | bytes 388
  6.5 99.6 %all-reduce.3.cloned.1.call-start = ((), (), s32[]{:S(2)}) async-start(), calls=%async_computation.1 | async-start | bytes 2097152 | tf_op jit(solution)/shard_map/psum | solution.py:19
  10.3 125.7 %reduce-scatter.2.cloned.1.call-start = ((), (), s32[]{:S(2)}) async-start(), calls=%async_computation.2 | async-start | bytes 983040 | tf_op jit(solution)/shard_map/reduce_scatter | solution.py:25
  109.0 9.4 %copy-start = (f32[2048,128]{1,0:T(8,128)S(1)}, f32[2048,128]{1,0:T(8,128)}, u32[]{:S(2)}) copy-start(f32[2048,128]{1,0:T(8,128)} %all-reduce.3.cloned.1.call-done) | copy-start | bytes 3145732
  121.2 154.9 %all-reduce.5.cloned.1.call-start = ((), (), s32[]{:S(2)}) async-start(), calls=%async_computation.3 | async-start | bytes 655360 | tf_op jit(solution)/shard_map/psum | solution.py:26
Sparse Core Ops, SparseCore 0:
  10.4 95.6 all-reduce.2
  121.3 14.6 reduce-scatter.1
  138.6 137.4 all-reduce.4

commit v2 on v1

v2 whole, which is shorter than its diff:
```python
import functools

import jax
import jax.numpy as jnp
from jax import lax
from jax.experimental import pallas as pl
from jax.experimental.pallas import tpu as pltpu
from jax.sharding import PartitionSpec as P

MESH = pl.DeviceIdType.MESH
HIGH = lax.Precision.HIGHEST
EDGE = 64
PAIRS = 8
RETURNED = (0, 3, 5)
CROSSED_FIRST = (1, 4, 6)
LAG = 2


def one_of(i, members):
    hit = i == members[0]
    for m in members[1:]:
        hit = jnp.logical_or(hit, i == m)
    return hit


def gather_kernel(tiles, mask, dest, out, wide, pan, acc, got, front, part, full, load_sem, send_sem, recv_sem, leaf_sem, rs_sem, ag_sem):
    leaf = lax.axis_index("leaf")
    row = lax.axis_index("row")
    col = lax.axis_index("col")
    y = col // 2
    mine = col % 2
    other = 1 - mine
    rows_n = lax.axis_size("row")

    def at(y_to, x_to):
        return (leaf, row, lax.rem(y_to + 4, 4) * 2 + x_to)

    up, down, across = at(y + 1, mine), at(y - 1, mine), at(y, other)
    peer = lambda j: (leaf, lax.rem(row + j, rows_n), col)
    partner = (1 - leaf, row, col)

    lanes = 128
    loads = []
    for b in range(4):
        span = pl.ds(b * lanes, lanes)
        loads.append(pltpu.make_async_copy(tiles.at[:, :, span], wide.at[:, :, span], load_sem.at[b]))
        loads[-1].start()

    barrier = pltpu.get_barrier_semaphore()
    targets = [up, down, across, partner] + [peer(j) for j in range(1, 16)]
    for t in targets:
        pl.semaphore_signal(barrier, inc=1, device_id=t, device_id_type=MESH)

    expand = (lax.broadcasted_iota(jnp.int32, (8, 512), 1) // EDGE == lax.broadcasted_iota(jnp.int32, (8, 512), 0)).astype(jnp.float32)
    maskw = jnp.dot(mask[...].astype(jnp.float32), expand, preferred_element_type=jnp.float32)
    in_first = (dest[...] < 16).astype(jnp.float32)
    place = (lax.broadcasted_iota(jnp.int32, (32, 2048), 1) // EDGE == lax.broadcasted_iota(jnp.int32, (32, 2048), 0)).astype(jnp.float32)
    first = jnp.sum(place * in_first, axis=0, keepdims=True)
    for k in range(PAIRS):
        front[k] = jnp.broadcast_to(first[:, k * 256:(k + 1) * 256], (8, 256))
    for t in range(32):
        got[t] = jnp.broadcast_to(maskw[t:t + 1], (8, 512))

    def copy_of(p, c, way, to):
        return pltpu.make_async_remote_copy(
            src_ref=pan.at[p, c], dst_ref=pan.at[p, c], send_sem=send_sem.at[way, p, c],
            recv_sem=recv_sem.at[p, c], device_id=to, device_id_type=MESH)

    def forward(i, d, act):
        c = 2 * i + d
        step = y if d == 0 else lax.rem(4 - y, 4)
        ahead, back = (up, down) if d == 0 else (down, up)
        returned, crossed = one_of(i, RETURNED), one_of(i, CROSSED_FIRST)
        del back

        @pl.when(step < 3)
        def _():
            act(copy_of(mine, c, 0, ahead))

        later = jnp.logical_and(step > 0, jnp.logical_not(crossed))
        now = jnp.logical_and(step == 0, jnp.logical_not(returned))

        @pl.when(jnp.logical_or(later, now))
        def _():
            act(copy_of(mine, c, 1, across))

    def forward_other(i, d, act):
        c = 2 * i + d
        step = y if d == 0 else lax.rem(4 - y, 4)
        ahead, back = (up, down) if d == 0 else (down, up)
        returned, crossed = one_of(i, RETURNED), one_of(i, CROSSED_FIRST)

        @pl.when(jnp.logical_and(crossed, step < 3))
        def _():
            act(copy_of(other, c, 0, ahead))

        @pl.when(jnp.logical_and(returned, step == 1))
        def _():
            act(copy_of(other, c, 0, back))

    start = lambda cp: cp.start()
    drain = lambda cp: cp.wait_send()

    loads[0].wait()
    pl.semaphore_wait(barrier, len(targets))

    @pl.when(y == 0)
    def _():
        def pack(i, carry):
            for d in range(2):
                c = 2 * i + d
                two = []
                for t in range(2):
                    tile = 2 * c + t
                    two.append(wide[tile, :, 0:lanes] * got[tile, 0:1, 0:lanes])
                flat = jnp.concatenate(two, axis=0)
                pan[mine, c] = flat.T[0:EDGE, :]
                forward(i, d, start)
            return carry

        lax.fori_loop(0, PAIRS, pack, 0)

    acc[...] = jnp.zeros_like(acc)
    for b in range(1, 4):
        loads[b].wait()

    def step_fn(i, carry):
        @pl.when(jnp.logical_and(i < PAIRS, y > 0))
        def _():
            for d in range(2):
                copy_of(mine, 2 * i + d, 0, up).wait_recv()
                forward(i, d, start)

        @pl.when(i >= LAG)
        def _():
            k = i - LAG
            for d in range(2):
                copy_of(other, 2 * k + d, 0, up).wait_recv()
                forward_other(k, d, start)
            right = []
            for t in range(4):
                tile = 4 * k + t
                right.append(wide[tile] * got[tile, 0:1, :])
            right = jnp.concatenate(right, axis=0)
            left = jnp.concatenate(
                [jnp.concatenate([pan[p, 2 * k], pan[p, 2 * k + 1]], axis=1) for p in range(2)], axis=0)
            sel = front[k, 0:1, :]
            both = jnp.concatenate([left * sel, left * (1.0 - sel)], axis=0)
            acc[:, 0:512] += jnp.dot(both, right, precision=HIGH, preferred_element_type=jnp.float32)
            acc[:, 512:640] += lax.dot_general(both, left, (((1,), (1,)), ((), ())), precision=HIGH, preferred_element_type=jnp.float32)

        return carry

    lax.fori_loop(0, PAIRS + LAG, step_fn, 0)

    give = pltpu.make_async_remote_copy(
        src_ref=acc.at[pl.ds(pl.multiple_of((1 - leaf) * 128, 128), 128)], dst_ref=part, send_sem=leaf_sem.at[0],
        recv_sem=leaf_sem.at[1], device_id=partner, device_id_type=MESH)
    give.start()
    give.wait_recv()
    own = pl.ds(pl.multiple_of(leaf * 128, 128), 128)
    acc[own] = acc[own] + part[...]

    def piece(j):
        return pl.ds(pl.multiple_of(leaf * 128 + j * 8, 8), 8)

    scat = []
    for j in range(1, 16):
        cp = pltpu.make_async_remote_copy(
            src_ref=acc.at[piece(lax.rem(row + j, rows_n))], dst_ref=full.at[1, pl.ds(j * 8, 8)], send_sem=rs_sem.at[0, j],
            recv_sem=rs_sem.at[1, j], device_id=peer(j), device_id_type=MESH)
        cp.start()
        scat.append(cp)
    total = acc[piece(row)]
    for j, cp in enumerate(scat):
        cp.wait_recv()
        total = total + full[1, pl.ds((j + 1) * 8, 8)]
    slot = pl.ds(pl.multiple_of(row * 8, 8), 8)
    full[0, slot] = total
    spread = []
    for j in range(1, 16):
        cp = pltpu.make_async_remote_copy(
            src_ref=full.at[0, slot], dst_ref=full.at[0, slot], send_sem=ag_sem.at[0, j],
            recv_sem=ag_sem.at[1, j], device_id=peer(j), device_id_type=MESH)
        cp.start()
        spread.append(cp)
    for cp in spread:
        cp.wait_recv()
    out[...] = full[0]

    give.wait_send()
    for cp in scat + spread:
        cp.wait_send()

    def finish(i, carry):
        for d in range(2):
            forward(i, d, drain)
            forward_other(i, d, drain)
        return carry

    lax.fori_loop(0, PAIRS, finish, 0)


def inverse_lower(d):
    n = d.shape[0]
    lane = lax.broadcasted_iota(jnp.int32, (n, 128), 1)
    line = lax.broadcasted_iota(jnp.int32, (n, 128), 0)
    cols = [jnp.broadcast_to(d[:, k:k + 1], (n, 128)) for k in range(n)]
    x = (lane == line).astype(jnp.float32)
    pivots = jnp.ones((n, 128), jnp.float32)
    for j in range(n):
        pivot = cols[j][j:j + 1, :]
        m = jnp.where(line > j, cols[j] * (1.0 / pivot), 0.0)
        for k in range(j + 1, n):
            cols[k] = cols[k] - m * cols[k][j:j + 1, :]
        x = x - m * x[j:j + 1, :]
        pivots = jnp.where(line == j, pivot, pivots)
    return (x / jnp.sqrt(pivots))[:, 0:n]


def solve_kernel(sums, out):
    col = lax.axis_index("col")
    n = 32
    rest = sums[...]
    done = []
    for b in range(4):
        at = 512 + b * n
        low = inverse_lower(rest[0:n, at:at + n])
        lead = jnp.dot(low, rest[0:n], precision=HIGH, preferred_element_type=jnp.float32)
        done.append(lead[:, 0:512])
        if b < 3:
            left = lead[:, at + n:640]
            rest = rest[n:] - lax.dot_general(left, lead, (((0,), (0,)), ((), ())), precision=HIGH, preferred_element_type=jnp.float32)
    top = jnp.concatenate(done, axis=0)
    place = (lax.broadcasted_iota(jnp.int32, (128, 512), 1) // EDGE) * 8 + col
    line = lax.broadcasted_iota(jnp.int32, (128, 512), 0) // EDGE
    out[0] = jnp.where(place >= line, top, 0.0)


def per_device(tiles, mask, dest):
    vmem = pl.BlockSpec(memory_space=pltpu.VMEM)
    dma = pltpu.SemaphoreType.DMA
    sums = pl.pallas_call(
        gather_kernel,
        out_shape=jax.ShapeDtypeStruct((128, 640), jnp.float32),
        in_specs=[pl.BlockSpec(memory_space=pl.ANY), vmem, vmem],
        out_specs=vmem,
        scratch_shapes=[
            pltpu.VMEM((32, 64, 512), jnp.float32),
            pltpu.VMEM((2, 16, 64, 128), jnp.float32),
            pltpu.VMEM((256, 640), jnp.float32),
            pltpu.VMEM((32, 8, 512), jnp.float32),
            pltpu.VMEM((PAIRS, 8, 256), jnp.float32),
            pltpu.VMEM((128, 640), jnp.float32),
            pltpu.VMEM((2, 128, 640), jnp.float32),
            dma((4,)), dma((2, 2, 16)), dma((2, 16)), dma((2,)), dma((2, 16)), dma((2, 16)),
        ],
        compiler_params=pltpu.CompilerParams(collective_id=0, has_side_effects=True),
    )(tiles, mask, dest)
    return pl.pallas_call(
        solve_kernel,
        out_shape=jax.ShapeDtypeStruct((1, 128, 512), jnp.float32),
        in_specs=[vmem],
        out_specs=vmem,
    )(sums)


def solution(mesh):
    in_specs = (
        P(("leaf", "row"), None, "col"),
        P(("leaf", "row"), "col"),
        P(("leaf", "row"), None),
    )
    return jax.shard_map(
        per_device, mesh=mesh, in_specs=in_specs, out_specs=P("leaf", None, "col"), check_vma=False
    )
```

time: 310 us -> 185 us (0.60)
  the two profiles are of different devices: /device:TPU:6 before, /device:TPU:9 now
where the time goes in v2:
time: 185 us
  Pallas kernels  182 us (98%)
  local copies, waits for them, and re-layouts  2.7 us (1%)
    pallas_call x1, Pallas kernels, per_device(): pl.pallas_call(gather_kernel, out_shape=jax.ShapeDtypeStruct((128, 640),...  175 us
    pallas_call x1, Pallas kernels, per_device(): pl.pallas_call(solve_kernel, out_shape=jax.ShapeDtypeStruct((1, 128, 512)...  6.97 us

profile of v2, /device:TPU:9, one launch (start us, length us, event | category | flops | bytes accessed | tf_op | source)
XLA Modules:
  0.0 185.1 jit_solution(15244691416604084574)
XLA Ops:
  0.0 1.4 copy.4.mask
  1.4 1.3 copy.5.dest
  2.7 175.4 %shard_map.37.sums = f32[128,640]{1,0:T(8,128)} custom-call(f32[32,64,512]{2,1,0:T(8,128)} %tiles.1, s32[32,8]{1,0:T(8,128)} %copy.4.mask, s32[32,1]{1,0:T(8,128)} %copy.5.dest), custom_call_target="tpu_custom_call" | custom-call | tf_op jit(solution)/shard_map/pallas_call | solution.py:243
  178.1 7.0 %shard_map.38 = f32[1,128,512]{2,1,0:T(8,128)} custom-call(f32[128,640]{1,0:T(8,128)} %shard_map.37.sums), custom_call_target="tpu_custom_call" | custom-call | tf_op jit(solution)/shard_map/pallas_call | solution.py:260

commit v3 on v2

--- a/solution.py
+++ b/solution.py
@@ -11,16 +11,8 @@
 HIGH = lax.Precision.HIGHEST
 EDGE = 64
 PAIRS = 8
-RETURNED = (0, 3, 5)
-CROSSED_FIRST = (1, 4, 6)
-LAG = 2
-
-
-def one_of(i, members):
-    hit = i == members[0]
-    for m in members[1:]:
-        hit = jnp.logical_or(hit, i == m)
-    return hit
+CHUNKS = 16
+LAG = 6
 
 
 def gather_kernel(tiles, mask, dest, out, wide, pan, acc, got, front, part, full, load_sem, send_sem, recv_sem, leaf_sem, rs_sem, ag_sem):
@@ -36,6 +28,7 @@
         return (leaf, row, lax.rem(y_to + 4, 4) * 2 + x_to)
 
     up, down, across = at(y + 1, mine), at(y - 1, mine), at(y, other)
+    middle = at(2, mine)
     peer = lambda j: (leaf, lax.rem(row + j, rows_n), col)
     partner = (1 - leaf, row, col)
 
@@ -51,13 +44,15 @@
     for t in targets:
         pl.semaphore_signal(barrier, inc=1, device_id=t, device_id_type=MESH)
 
-    expand = (lax.broadcasted_iota(jnp.int32, (8, 512), 1) // EDGE == lax.broadcasted_iota(jnp.int32, (8, 512), 0)).astype(jnp.float32)
-    maskw = jnp.dot(mask[...].astype(jnp.float32), expand, preferred_element_type=jnp.float32)
-    in_first = (dest[...] < 16).astype(jnp.float32)
-    place = (lax.broadcasted_iota(jnp.int32, (32, 2048), 1) // EDGE == lax.broadcasted_iota(jnp.int32, (32, 2048), 0)).astype(jnp.float32)
-    first = jnp.sum(place * in_first, axis=0, keepdims=True)
+    def blocks_of(rows_, width):
+        shape = (rows_, width)
+        return (lax.broadcasted_iota(jnp.int32, shape, 1) // EDGE == lax.broadcasted_iota(jnp.int32, shape, 0)).astype(jnp.float32)
+
+    maskw = lax.dot_general(mask[...].astype(jnp.float32), blocks_of(8, 512), (((0,), (0,)), ((), ())), preferred_element_type=jnp.float32)
+    in_first = jnp.broadcast_to((dest[...] < 16).astype(jnp.float32), (8, 32))
+    first = jnp.dot(in_first, blocks_of(32, 2048), preferred_element_type=jnp.float32)
     for k in range(PAIRS):
-        front[k] = jnp.broadcast_to(first[:, k * 256:(k + 1) * 256], (8, 256))
+        front[k] = first[:, k * 256:(k + 1) * 256]
     for t in range(32):
         got[t] = jnp.broadcast_to(maskw[t:t + 1], (8, 512))
 
@@ -66,37 +61,29 @@
             src_ref=pan.at[p, c], dst_ref=pan.at[p, c], send_sem=send_sem.at[way, p, c],
             recv_sem=recv_sem.at[p, c], device_id=to, device_id_type=MESH)
 
-    def forward(i, d, act):
-        c = 2 * i + d
-        step = y if d == 0 else lax.rem(4 - y, 4)
-        ahead, back = (up, down) if d == 0 else (down, up)
-        returned, crossed = one_of(i, RETURNED), one_of(i, CROSSED_FIRST)
-        del back
-
-        @pl.when(step < 3)
-        def _():
-            act(copy_of(mine, c, 0, ahead))
-
-        later = jnp.logical_and(step > 0, jnp.logical_not(crossed))
-        now = jnp.logical_and(step == 0, jnp.logical_not(returned))
-
-        @pl.when(jnp.logical_or(later, now))
-        def _():
-            act(copy_of(mine, c, 1, across))
-
-    def forward_other(i, d, act):
-        c = 2 * i + d
-        step = y if d == 0 else lax.rem(4 - y, 4)
-        ahead, back = (up, down) if d == 0 else (down, up)
-        returned, crossed = one_of(i, RETURNED), one_of(i, CROSSED_FIRST)
-
-        @pl.when(jnp.logical_and(crossed, step < 3))
-        def _():
-            act(copy_of(other, c, 0, ahead))
-
-        @pl.when(jnp.logical_and(returned, step == 1))
-        def _():
-            act(copy_of(other, c, 0, back))
+    edge_y = y == 0
+    relay_y = lax.rem(y, 2) == 1
+
+    def sends(c, act):
+        half = jnp.logical_and(relay_y, lax.rem(c, 2) == y // 2)
+
+        @pl.when(jnp.logical_or(edge_y, relay_y))
+        def _():
+            act(copy_of(mine, c, 0, across))
+
+        @pl.when(edge_y)
+        def _():
+            act(copy_of(mine, c, 1, up))
+            act(copy_of(mine, c, 2, down))
+
+        @pl.when(half)
+        def _():
+            act(copy_of(mine, c, 1, middle))
+
+    def sends_other(c, act):
+        @pl.when(jnp.logical_and(relay_y, lax.rem(c, 2) == y // 2))
+        def _():
+            act(copy_of(other, c, 0, middle))
 
     start = lambda cp: cp.start()
     drain = lambda cp: cp.wait_send()
@@ -106,37 +93,38 @@
 
     @pl.when(y == 0)
     def _():
-        def pack(i, carry):
-            for d in range(2):
-                c = 2 * i + d
-                two = []
-                for t in range(2):
-                    tile = 2 * c + t
-                    two.append(wide[tile, :, 0:lanes] * got[tile, 0:1, 0:lanes])
-                flat = jnp.concatenate(two, axis=0)
-                pan[mine, c] = flat.T[0:EDGE, :]
-                forward(i, d, start)
+        def pack(c, carry):
+            two = [wide[2 * c + t, :, 0:lanes] * got[2 * c + t, 0:1, 0:lanes] for t in range(2)]
+            pan[mine, c] = jnp.concatenate(two, axis=0).T[0:EDGE, :]
+            sends(c, start)
             return carry
 
-        lax.fori_loop(0, PAIRS, pack, 0)
+        lax.fori_loop(0, CHUNKS, pack, 0)
 
     acc[...] = jnp.zeros_like(acc)
     for b in range(1, 4):
         loads[b].wait()
 
     def step_fn(i, carry):
-        @pl.when(jnp.logical_and(i < PAIRS, y > 0))
-        def _():
-            for d in range(2):
-                copy_of(mine, 2 * i + d, 0, up).wait_recv()
-                forward(i, d, start)
+        @pl.when(jnp.logical_and(i < CHUNKS, relay_y))
+        def _():
+            copy_of(mine, i, 0, up).wait_recv()
+            sends(i, start)
 
         @pl.when(i >= LAG)
         def _():
-            k = i - LAG
-            for d in range(2):
-                copy_of(other, 2 * k + d, 0, up).wait_recv()
-                forward_other(k, d, start)
+            c = i - LAG
+
+            @pl.when(y == 2)
+            def _():
+                copy_of(mine, c, 0, up).wait_recv()
+
+            copy_of(other, c, 0, up).wait_recv()
+            sends_other(c, start)
+
+        @pl.when(jnp.logical_and(i >= LAG, lax.rem(i - LAG, 2) == 1))
+        def _():
+            k = (i - LAG) // 2
             right = []
             for t in range(4):
                 tile = 4 * k + t
@@ -151,7 +139,7 @@
 
         return carry
 
-    lax.fori_loop(0, PAIRS + LAG, step_fn, 0)
+    lax.fori_loop(0, CHUNKS + LAG, step_fn, 0)
 
     give = pltpu.make_async_remote_copy(
         src_ref=acc.at[pl.ds(pl.multiple_of((1 - leaf) * 128, 128), 128)], dst_ref=part, send_sem=leaf_sem.at[0],
@@ -192,13 +180,12 @@
     for cp in scat + spread:
         cp.wait_send()
 
-    def finish(i, carry):
-        for d in range(2):
-            forward(i, d, drain)
-            forward_other(i, d, drain)
+    def finish(c, carry):
+        sends(c, drain)
+        sends_other(c, drain)
         return carry
 
-    lax.fori_loop(0, PAIRS, finish, 0)
+    lax.fori_loop(0, CHUNKS, finish, 0)
 
 
 def inverse_lower(d):
@@ -253,10 +240,10 @@
             pltpu.VMEM((PAIRS, 8, 256), jnp.float32),
             pltpu.VMEM((128, 640), jnp.float32),
             pltpu.VMEM((2, 128, 640), jnp.float32),
-            dma((4,)), dma((2, 2, 16)), dma((2, 16)), dma((2,)), dma((2, 16)), dma((2, 16)),
+            dma((4,)), dma((3, 2, CHUNKS)), dma((2, CHUNKS)), dma((2,)), dma((2, 16)), dma((2, 16)),
         ],
         compiler_params=pltpu.CompilerParams(collective_id=0, has_side_effects=True),
-    )(tiles, mask, dest)
+    )(tiles, mask.T, dest.T)
     return pl.pallas_call(
         solve_kernel,
         out_shape=jax.ShapeDtypeStruct((1, 128, 512), jnp.float32),

time: 185 us -> 60.8 us (0.33)
  the two profiles are of different devices: /device:TPU:9 before, /device:TPU:17 now
where the time goes in v3:
time: 60.8 us; the launch traced here: 60.7 us
  Pallas kernels  60.7 us (100%)
    pallas_call x1, Pallas kernels, per_device(): pl.pallas_call(gather_kernel, out_shape=jax.ShapeDtypeStruct((128, 640),...  53.7 us
    pallas_call x1, Pallas kernels, per_device(): pl.pallas_call(solve_kernel, out_shape=jax.ShapeDtypeStruct((1, 128, 512)...  6.97 us

profile of v3, /device:TPU:17, one launch (start us, length us, event | category | flops | bytes accessed | tf_op | source)
XLA Modules:
  0.0 60.7 jit_solution(5009859056158828178)
XLA Ops:
  0.0 53.7 %shard_map.37.sums = f32[128,640]{1,0:T(8,128)} custom-call(f32[32,64,512]{2,1,0:T(8,128)} %tiles.1, s32[8,32]{1,0:T(8,128)} %bitcast.2, s32[1,32]{1,0:T(1,128)} %bitcast.3), custom_call_target="tpu_custom_call" | custom-call | tf_op jit(solution)/shard_map/pallas_call | solution.py:230
  53.7 7.0 %shard_map.38 = f32[1,128,512]{2,1,0:T(8,128)} custom-call(f32[128,640]{1,0:T(8,128)} %shard_map.37.sums), custom_call_target="tpu_custom_call" | custom-call | tf_op jit(solution)/shard_map/pallas_call | solution.py:247

commit v4 on v3

--- a/solution.py
+++ b/solution.py
@@ -13,9 +13,10 @@
 PAIRS = 8
 CHUNKS = 16
 LAG = 6
-
-
-def gather_kernel(tiles, mask, dest, out, wide, pan, acc, got, front, part, full, load_sem, send_sem, recv_sem, leaf_sem, rs_sem, ag_sem):
+FAR_FIRST = (8, 7, 9, 6, 10, 5, 11, 4, 12, 3, 13, 2, 14, 1, 15)
+
+
+def gather_kernel(tiles, mask, dest, out, wide, pan, acc, gram, got, front, part, part_g, come, come_g, full, full_g, load_sem, send_sem, recv_sem, leaf_sem, rs_sem, ag_sem):
     leaf = lax.axis_index("leaf")
     row = lax.axis_index("row")
     col = lax.axis_index("col")
@@ -37,7 +38,7 @@
     for b in range(4):
         span = pl.ds(b * lanes, lanes)
         loads.append(pltpu.make_async_copy(tiles.at[:, :, span], wide.at[:, :, span], load_sem.at[b]))
-        loads[-1].start()
+    loads[0].start()
 
     barrier = pltpu.get_barrier_semaphore()
     targets = [up, down, across, partner] + [peer(j) for j in range(1, 16)]
@@ -85,6 +86,8 @@
         def _():
             act(copy_of(other, c, 0, middle))
 
+    for b in range(1, 4):
+        loads[b].start()
     start = lambda cp: cp.start()
     drain = lambda cp: cp.wait_send()
 
@@ -102,6 +105,7 @@
         lax.fori_loop(0, CHUNKS, pack, 0)
 
     acc[...] = jnp.zeros_like(acc)
+    gram[...] = jnp.zeros_like(gram)
     for b in range(1, 4):
         loads[b].wait()
 
@@ -134,50 +138,63 @@
                 [jnp.concatenate([pan[p, 2 * k], pan[p, 2 * k + 1]], axis=1) for p in range(2)], axis=0)
             sel = front[k, 0:1, :]
             both = jnp.concatenate([left * sel, left * (1.0 - sel)], axis=0)
-            acc[:, 0:512] += jnp.dot(both, right, precision=HIGH, preferred_element_type=jnp.float32)
-            acc[:, 512:640] += lax.dot_general(both, left, (((1,), (1,)), ((), ())), precision=HIGH, preferred_element_type=jnp.float32)
+            gram[...] += lax.dot_general(both, left, (((1,), (1,)), ((), ())), precision=HIGH, preferred_element_type=jnp.float32)
+            for h in range(2):
+                acc[h] += jnp.dot(both, right[:, h * 256:(h + 1) * 256], precision=HIGH, preferred_element_type=jnp.float32)
 
         return carry
 
     lax.fori_loop(0, CHUNKS + LAG, step_fn, 0)
 
-    give = pltpu.make_async_remote_copy(
-        src_ref=acc.at[pl.ds(pl.multiple_of((1 - leaf) * 128, 128), 128)], dst_ref=part, send_sem=leaf_sem.at[0],
-        recv_sem=leaf_sem.at[1], device_id=partner, device_id_type=MESH)
-    give.start()
-    give.wait_recv()
-    own = pl.ds(pl.multiple_of(leaf * 128, 128), 128)
-    acc[own] = acc[own] + part[...]
+    other_rows = pl.ds(pl.multiple_of((1 - leaf) * 128, 128), 128)
+    own_rows = pl.ds(pl.multiple_of(leaf * 128, 128), 128)
+    slot = pl.ds(pl.multiple_of(row * 8, 8), 8)
+
+    def remote(src, dst, sems, n, to):
+        cp = pltpu.make_async_remote_copy(
+            src_ref=src, dst_ref=dst, send_sem=sems.at[(0,) + n], recv_sem=sems.at[(1,) + n], device_id=to, device_id_type=MESH)
+        cp.start()
+        return cp
+
+    sums = [gram, acc.at[0], acc.at[1]]
+    parts = [part_g, part.at[0], part.at[1]]
+    comes = [come_g, come.at[0], come.at[1]]
+    fulls = [full_g, full.at[0], full.at[1]]
+    gives = [remote(sums[t].at[other_rows], parts[t], leaf_sem, (t,), partner) for t in range(3)]
+    sent = list(gives)
 
     def piece(j):
-        return pl.ds(pl.multiple_of(leaf * 128 + j * 8, 8), 8)
-
-    scat = []
-    for j in range(1, 16):
-        cp = pltpu.make_async_remote_copy(
-            src_ref=acc.at[piece(lax.rem(row + j, rows_n))], dst_ref=full.at[1, pl.ds(j * 8, 8)], send_sem=rs_sem.at[0, j],
-            recv_sem=rs_sem.at[1, j], device_id=peer(j), device_id_type=MESH)
-        cp.start()
-        scat.append(cp)
-    total = acc[piece(row)]
-    for j, cp in enumerate(scat):
+        return pl.ds(pl.multiple_of(leaf * 128 + lax.rem(row + j, rows_n) * 8, 8), 8)
+
+    scats = []
+    for t in range(3):
+        gives[t].wait_recv()
+        sums[t][own_rows] = sums[t][own_rows] + parts[t][...]
+        scats.append([remote(sums[t].at[piece(j)], comes[t].at[j], rs_sem, (t, j), peer(j)) for j in FAR_FIRST])
+        sent += scats[t]
+    spreads = []
+    for t in range(3):
+        for cp in scats[t]:
+            cp.wait_recv()
+        total = sums[t][piece(0)]
+        for j in range(1, 16):
+            total = total + comes[t][j]
+        fulls[t][slot] = total
+        spreads.append([remote(fulls[t].at[slot], fulls[t].at[slot], ag_sem, (t, j), peer(j)) for j in FAR_FIRST])
+        sent += spreads[t]
+
+    for cp in spreads[0]:
         cp.wait_recv()
-        total = total + full[1, pl.ds((j + 1) * 8, 8)]
-    slot = pl.ds(pl.multiple_of(row * 8, 8), 8)
-    full[0, slot] = total
-    spread = []
-    for j in range(1, 16):
-        cp = pltpu.make_async_remote_copy(
-            src_ref=full.at[0, slot], dst_ref=full.at[0, slot], send_sem=ag_sem.at[0, j],
-            recv_sem=ag_sem.at[1, j], device_id=peer(j), device_id_type=MESH)
-        cp.start()
-        spread.append(cp)
-    for cp in spread:
-        cp.wait_recv()
-    out[...] = full[0]
-
-    give.wait_send()
-    for cp in scat + spread:
+    low = inverse_of_factor(full_g[...])
+    line = lax.broadcasted_iota(jnp.int32, (128, 256), 0) // EDGE
+    for h in range(2):
+        for cp in spreads[1 + h]:
+            cp.wait_recv()
+        top = jnp.dot(low, full[h], precision=HIGH, preferred_element_type=jnp.float32)
+        place = (lax.broadcasted_iota(jnp.int32, (128, 256), 1) // EDGE + 4 * h) * 8 + col
+        out[0, :, h * 256:(h + 1) * 256] = jnp.where(place >= line, top, 0.0)
+
+    for cp in sent:
         cp.wait_send()
 
     def finish(c, carry):
@@ -205,51 +222,48 @@
     return (x / jnp.sqrt(pivots))[:, 0:n]
 
 
-def solve_kernel(sums, out):
-    col = lax.axis_index("col")
+def inverse_of_factor(g):
     n = 32
-    rest = sums[...]
+    size = g.shape[0]
+    eye = (lax.broadcasted_iota(jnp.int32, g.shape, 0) == lax.broadcasted_iota(jnp.int32, g.shape, 1)).astype(jnp.float32)
+    rest = jnp.concatenate([eye, g], axis=1)
     done = []
-    for b in range(4):
-        at = 512 + b * n
+    for b in range(size // n):
+        at = size + b * n
         low = inverse_lower(rest[0:n, at:at + n])
         lead = jnp.dot(low, rest[0:n], precision=HIGH, preferred_element_type=jnp.float32)
-        done.append(lead[:, 0:512])
-        if b < 3:
-            left = lead[:, at + n:640]
+        done.append(lead[:, 0:size])
+        if b + 1 < size // n:
+            left = lead[:, at + n:2 * size]
             rest = rest[n:] - lax.dot_general(left, lead, (((0,), (0,)), ((), ())), precision=HIGH, preferred_element_type=jnp.float32)
-    top = jnp.concatenate(done, axis=0)
-    place = (lax.broadcasted_iota(jnp.int32, (128, 512), 1) // EDGE) * 8 + col
-    line = lax.broadcasted_iota(jnp.int32, (128, 512), 0) // EDGE
-    out[0] = jnp.where(place >= line, top, 0.0)
+    return jnp.concatenate(done, axis=0)
 
 
 def per_device(tiles, mask, dest):
     vmem = pl.BlockSpec(memory_space=pltpu.VMEM)
     dma = pltpu.SemaphoreType.DMA
-    sums = pl.pallas_call(
+    return pl.pallas_call(
         gather_kernel,
-        out_shape=jax.ShapeDtypeStruct((128, 640), jnp.float32),
+        out_shape=jax.ShapeDtypeStruct((1, 128, 512), jnp.float32),
         in_specs=[pl.BlockSpec(memory_space=pl.ANY), vmem, vmem],
         out_specs=vmem,
         scratch_shapes=[
             pltpu.VMEM((32, 64, 512), jnp.float32),
-            pltpu.VMEM((2, 16, 64, 128), jnp.float32),
-            pltpu.VMEM((256, 640), jnp.float32),
+            pltpu.VMEM((2, CHUNKS, 64, 128), jnp.float32),
+            pltpu.VMEM((2, 256, 256), jnp.float32),
+            pltpu.VMEM((256, 128), jnp.float32),
             pltpu.VMEM((32, 8, 512), jnp.float32),
             pltpu.VMEM((PAIRS, 8, 256), jnp.float32),
-            pltpu.VMEM((128, 640), jnp.float32),
-            pltpu.VMEM((2, 128, 640), jnp.float32),
-            dma((4,)), dma((3, 2, CHUNKS)), dma((2, CHUNKS)), dma((2,)), dma((2, 16)), dma((2, 16)),
+            pltpu.VMEM((2, 128, 256), jnp.float32),
+            pltpu.VMEM((128, 128), jnp.float32),
+            pltpu.VMEM((2, 16, 8, 256), jnp.float32),
+            pltpu.VMEM((16, 8, 128), jnp.float32),
+            pltpu.VMEM((2, 128, 256), jnp.float32),
+            pltpu.VMEM((128, 128), jnp.float32),
+            dma((4,)), dma((3, 2, CHUNKS)), dma((2, CHUNKS)), dma((2, 3)), dma((2, 3, 16)), dma((2, 3, 16)),
         ],
         compiler_params=pltpu.CompilerParams(collective_id=0, has_side_effects=True),
     )(tiles, mask.T, dest.T)
-    return pl.pallas_call(
-        solve_kernel,
-        out_shape=jax.ShapeDtypeStruct((1, 128, 512), jnp.float32),
-        in_specs=[vmem],
-        out_specs=vmem,
-    )(sums)
 
 
 def solution(mesh):

time: 60.8 us -> 54.2 us (0.89)
  Pallas kernels: 60.7 us -> 52.3 us
  local copies, waits for them, and re-layouts: 0 us -> 1.67 us
    pallas_call x2 -> x1, Pallas kernels: 60.7 us -> 52.3 us  [per_device(): pl.pallas_call(gather_kernel, out_shape=jax.ShapeDtypeStruct((1, 128, 512...]
    unnamed x0 -> x1, local copies, waits for them, and re-layouts: none -> 1.67 us
where the time goes in v4:
time: 54.2 us; the launch traced here: 54 us
  Pallas kernels  52.3 us (96%)
  local copies, waits for them, and re-layouts  1.67 us (3%)
    pallas_call x1, Pallas kernels, per_device(): pl.pallas_call(gather_kernel, out_shape=jax.ShapeDtypeStruct((1, 128, 512...  52.3 us
    unnamed x1, local copies, waits for them, and re-layouts  1.67 us

profile of v4, /device:TPU:17, one launch (start us, length us, event | category | flops | bytes accessed | tf_op | source)
XLA Modules:
  0.0 54.0 jit_solution(11233447693164291261)
XLA Ops:
  0.0 52.3 %shard_map.37 = f32[1,128,512]{2,1,0:T(8,128)} custom-call(f32[32,64,512]{2,1,0:T(8,128)} %tiles.1, s32[8,32]{1,0:T(8,128)} %bitcast.2, s32[1,32]{1,0:T(1,128)} %bitcast.3), custom_call_target="tpu_custom_call" | custom-call | tf_op jit(solution)/shard_map/pallas_call | solution.py:245
  52.3 1.7 %copy.5 = f32[1,128,512]{2,1,0:T(8,128)} copy(f32[1,128,512]{2,1,0:T(8,128)} %shard_map.37) | data formatting | bytes 524288

commit v5 on v4

--- a/solution.py
+++ b/solution.py
@@ -16,7 +16,15 @@
 FAR_FIRST = (8, 7, 9, 6, 10, 5, 11, 4, 12, 3, 13, 2, 14, 1, 15)
 
 
-def gather_kernel(tiles, mask, dest, out, wide, pan, acc, gram, got, front, part, part_g, come, come_g, full, full_g, load_sem, send_sem, recv_sem, leaf_sem, rs_sem, ag_sem):
+def split_dot(a, b):
+    a_high, b_high = a.astype(jnp.bfloat16), b.astype(jnp.bfloat16)
+    a_low = (a - a_high.astype(jnp.float32)).astype(jnp.bfloat16)
+    b_low = (b - b_high.astype(jnp.float32)).astype(jnp.bfloat16)
+    dot = functools.partial(jnp.dot, preferred_element_type=jnp.float32)
+    return dot(a_high, b_high) + (dot(a_low, b_high) + dot(a_high, b_low))
+
+
+def gather_kernel(tiles, mask_in, dest_in, out, mask, dest, wide, pan, acc, gram, got, front, part, part_g, come, come_g, full, full_g, load_sem, send_sem, recv_sem, leaf_sem, rs_sem, ag_sem):
     leaf = lax.axis_index("leaf")
     row = lax.axis_index("row")
     col = lax.axis_index("col")
@@ -40,6 +48,10 @@
         loads.append(pltpu.make_async_copy(tiles.at[:, :, span], wide.at[:, :, span], load_sem.at[b]))
     loads[0].start()
 
+    small = [pltpu.make_async_copy(mask_in, mask, load_sem.at[4]), pltpu.make_async_copy(dest_in, dest, load_sem.at[5])]
+    for cp in small:
+        cp.start()
+
     barrier = pltpu.get_barrier_semaphore()
     targets = [up, down, across, partner] + [peer(j) for j in range(1, 16)]
     for t in targets:
@@ -49,6 +61,8 @@
         shape = (rows_, width)
         return (lax.broadcasted_iota(jnp.int32, shape, 1) // EDGE == lax.broadcasted_iota(jnp.int32, shape, 0)).astype(jnp.float32)
 
+    for cp in small:
+        cp.wait()
     maskw = lax.dot_general(mask[...].astype(jnp.float32), blocks_of(8, 512), (((0,), (0,)), ((), ())), preferred_element_type=jnp.float32)
     in_first = jnp.broadcast_to((dest[...] < 16).astype(jnp.float32), (8, 32))
     first = jnp.dot(in_first, blocks_of(32, 2048), preferred_element_type=jnp.float32)
@@ -139,8 +153,7 @@
             sel = front[k, 0:1, :]
             both = jnp.concatenate([left * sel, left * (1.0 - sel)], axis=0)
             gram[...] += lax.dot_general(both, left, (((1,), (1,)), ((), ())), precision=HIGH, preferred_element_type=jnp.float32)
-            for h in range(2):
-                acc[h] += jnp.dot(both, right[:, h * 256:(h + 1) * 256], precision=HIGH, preferred_element_type=jnp.float32)
+            acc[...] += split_dot(both, right)
 
         return carry
 
@@ -156,24 +169,24 @@
         cp.start()
         return cp
 
-    sums = [gram, acc.at[0], acc.at[1]]
-    parts = [part_g, part.at[0], part.at[1]]
-    comes = [come_g, come.at[0], come.at[1]]
-    fulls = [full_g, full.at[0], full.at[1]]
-    gives = [remote(sums[t].at[other_rows], parts[t], leaf_sem, (t,), partner) for t in range(3)]
+    sums = [gram, acc]
+    parts = [part_g, part]
+    comes = [come_g, come]
+    fulls = [full_g, full]
+    gives = [remote(sums[t].at[other_rows], parts[t], leaf_sem, (t,), partner) for t in range(2)]
     sent = list(gives)
 
     def piece(j):
         return pl.ds(pl.multiple_of(leaf * 128 + lax.rem(row + j, rows_n) * 8, 8), 8)
 
     scats = []
-    for t in range(3):
+    for t in range(2):
         gives[t].wait_recv()
         sums[t][own_rows] = sums[t][own_rows] + parts[t][...]
         scats.append([remote(sums[t].at[piece(j)], comes[t].at[j], rs_sem, (t, j), peer(j)) for j in FAR_FIRST])
         sent += scats[t]
     spreads = []
-    for t in range(3):
+    for t in range(2):
         for cp in scats[t]:
             cp.wait_recv()
         total = sums[t][piece(0)]
@@ -186,13 +199,12 @@
     for cp in spreads[0]:
         cp.wait_recv()
     low = inverse_of_factor(full_g[...])
-    line = lax.broadcasted_iota(jnp.int32, (128, 256), 0) // EDGE
-    for h in range(2):
-        for cp in spreads[1 + h]:
-            cp.wait_recv()
-        top = jnp.dot(low, full[h], precision=HIGH, preferred_element_type=jnp.float32)
-        place = (lax.broadcasted_iota(jnp.int32, (128, 256), 1) // EDGE + 4 * h) * 8 + col
-        out[0, :, h * 256:(h + 1) * 256] = jnp.where(place >= line, top, 0.0)
+    line = lax.broadcasted_iota(jnp.int32, (128, 512), 0) // EDGE
+    place = (lax.broadcasted_iota(jnp.int32, (128, 512), 1) // EDGE) * 8 + col
+    for cp in spreads[1]:
+        cp.wait_recv()
+    top = jnp.dot(low, full[...], precision=HIGH, preferred_element_type=jnp.float32)
+    out[0] = jnp.where(place >= line, top, 0.0)
 
     for cp in sent:
         cp.wait_send()
@@ -245,22 +257,24 @@
     return pl.pallas_call(
         gather_kernel,
         out_shape=jax.ShapeDtypeStruct((1, 128, 512), jnp.float32),
-        in_specs=[pl.BlockSpec(memory_space=pl.ANY), vmem, vmem],
+        in_specs=[pl.BlockSpec(memory_space=pl.ANY)] * 3,
         out_specs=vmem,
         scratch_shapes=[
+            pltpu.VMEM((8, 32), jnp.int32),
+            pltpu.VMEM((1, 32), jnp.int32),
             pltpu.VMEM((32, 64, 512), jnp.float32),
             pltpu.VMEM((2, CHUNKS, 64, 128), jnp.float32),
-            pltpu.VMEM((2, 256, 256), jnp.float32),
+            pltpu.VMEM((256, 512), jnp.float32),
             pltpu.VMEM((256, 128), jnp.float32),
             pltpu.VMEM((32, 8, 512), jnp.float32),
             pltpu.VMEM((PAIRS, 8, 256), jnp.float32),
-            pltpu.VMEM((2, 128, 256), jnp.float32),
+            pltpu.VMEM((128, 512), jnp.float32),
             pltpu.VMEM((128, 128), jnp.float32),
-            pltpu.VMEM((2, 16, 8, 256), jnp.float32),
+            pltpu.VMEM((16, 8, 512), jnp.float32),
             pltpu.VMEM((16, 8, 128), jnp.float32),
-            pltpu.VMEM((2, 128, 256), jnp.float32),
+            pltpu.VMEM((128, 512), jnp.float32),
             pltpu.VMEM((128, 128), jnp.float32),
-            dma((4,)), dma((3, 2, CHUNKS)), dma((2, CHUNKS)), dma((2, 3)), dma((2, 3, 16)), dma((2, 3, 16)),
+            dma((6,)), dma((3, 2, CHUNKS)), dma((2, CHUNKS)), dma((2, 2)), dma((2, 2, 16)), dma((2, 2, 16)),
         ],
         compiler_params=pltpu.CompilerParams(collective_id=0, has_side_effects=True),
     )(tiles, mask.T, dest.T)

time: 54.2 us -> 52.4 us (0.967)
  Pallas kernels: 52.3 us -> 50.6 us
    pallas_call x1, Pallas kernels: 52.3 us -> 50.6 us  [per_device(): pl.pallas_call(gather_kernel, out_shape=jax.ShapeDtypeStruct((1, 128, 512...]
where the time goes in v5:
time: 52.4 us; the launch traced here: 52.3 us
  Pallas kernels  50.6 us (97%)
  local copies, waits for them, and re-layouts  1.67 us (3%)
    pallas_call x1, Pallas kernels, per_device(): pl.pallas_call(gather_kernel, out_shape=jax.ShapeDtypeStruct((1, 128, 512...  50.6 us
    unnamed x1, local copies, waits for them, and re-layouts  1.67 us

profile of v5, /device:TPU:17, one launch (start us, length us, event | category | flops | bytes accessed | tf_op | source)
XLA Modules:
  0.0 52.3 jit_solution(7653923798403593580)
XLA Ops:
  0.0 50.6 %shard_map.37 = f32[1,128,512]{2,1,0:T(8,128)} custom-call(f32[32,64,512]{2,1,0:T(8,128)} %tiles.1, s32[8,32]{1,0:T(8,128)} %bitcast.2, s32[1,32]{1,0:T(1,128)} %bitcast.3), custom_call_target="tpu_custom_call" | custom-call | tf_op jit(solution)/shard_map/pallas_call | solution.py:257
  50.6 1.7 %copy.5 = f32[1,128,512]{2,1,0:T(8,128)} copy(f32[1,128,512]{2,1,0:T(8,128)} %shard_map.37) | data formatting | bytes 524288

commit v6 on v5

--- a/solution.py
+++ b/solution.py
@@ -12,7 +12,7 @@
 EDGE = 64
 PAIRS = 8
 CHUNKS = 16
-LAG = 6
+LAG = 8
 FAR_FIRST = (8, 7, 9, 6, 10, 5, 11, 4, 12, 3, 13, 2, 14, 1, 15)
 
 
@@ -82,9 +82,7 @@
     def sends(c, act):
         half = jnp.logical_and(relay_y, lax.rem(c, 2) == y // 2)
 
-        @pl.when(jnp.logical_or(edge_y, relay_y))
-        def _():
-            act(copy_of(mine, c, 0, across))
+        act(copy_of(mine, c, 0, across))
 
         @pl.when(edge_y)
         def _():
@@ -94,11 +92,6 @@
         @pl.when(half)
         def _():
             act(copy_of(mine, c, 1, middle))
-
-    def sends_other(c, act):
-        @pl.when(jnp.logical_and(relay_y, lax.rem(c, 2) == y // 2))
-        def _():
-            act(copy_of(other, c, 0, middle))
 
     for b in range(1, 4):
         loads[b].start()
@@ -124,7 +117,7 @@
         loads[b].wait()
 
     def step_fn(i, carry):
-        @pl.when(jnp.logical_and(i < CHUNKS, relay_y))
+        @pl.when(jnp.logical_and(i < CHUNKS, y > 0))
         def _():
             copy_of(mine, i, 0, up).wait_recv()
             sends(i, start)
@@ -133,12 +126,7 @@
         def _():
             c = i - LAG
 
-            @pl.when(y == 2)
-            def _():
-                copy_of(mine, c, 0, up).wait_recv()
-
             copy_of(other, c, 0, up).wait_recv()
-            sends_other(c, start)
 
         @pl.when(jnp.logical_and(i >= LAG, lax.rem(i - LAG, 2) == 1))
         def _():
@@ -174,7 +162,6 @@
     comes = [come_g, come]
     fulls = [full_g, full]
     gives = [remote(sums[t].at[other_rows], parts[t], leaf_sem, (t,), partner) for t in range(2)]
-    sent = list(gives)
 
     def piece(j):
         return pl.ds(pl.multiple_of(leaf * 128 + lax.rem(row + j, rows_n) * 8, 8), 8)
@@ -184,7 +171,6 @@
         gives[t].wait_recv()
         sums[t][own_rows] = sums[t][own_rows] + parts[t][...]
         scats.append([remote(sums[t].at[piece(j)], comes[t].at[j], rs_sem, (t, j), peer(j)) for j in FAR_FIRST])
-        sent += scats[t]
     spreads = []
     for t in range(2):
         for cp in scats[t]:
@@ -194,11 +180,19 @@
             total = total + comes[t][j]
         fulls[t][slot] = total
         spreads.append([remote(fulls[t].at[slot], fulls[t].at[slot], ag_sem, (t, j), peer(j)) for j in FAR_FIRST])
-        sent += spreads[t]
-
+
+    def finish(c, carry):
+        sends(c, drain)
+        return carry
+
+    lax.fori_loop(0, CHUNKS, finish, 0)
+    for cp in gives + scats[0] + scats[1]:
+        cp.wait_send()
     for cp in spreads[0]:
         cp.wait_recv()
     low = inverse_of_factor(full_g[...])
+    for cp in spreads[0]:
+        cp.wait_send()
     line = lax.broadcasted_iota(jnp.int32, (128, 512), 0) // EDGE
     place = (lax.broadcasted_iota(jnp.int32, (128, 512), 1) // EDGE) * 8 + col
     for cp in spreads[1]:
@@ -206,15 +200,8 @@
     top = jnp.dot(low, full[...], precision=HIGH, preferred_element_type=jnp.float32)
     out[0] = jnp.where(place >= line, top, 0.0)
 
-    for cp in sent:
+    for cp in spreads[1]:
         cp.wait_send()
-
-    def finish(c, carry):
-        sends(c, drain)
-        sends_other(c, drain)
-        return carry
-
-    lax.fori_loop(0, CHUNKS, finish, 0)
 
 
 def inverse_lower(d):

time: 52.4 us -> 52.1 us (level)
  no operation moved by 1% of the time
where the time goes in v6:
time: 52.1 us; the launch traced here: 51.9 us
  Pallas kernels  50.2 us (96%)
  local copies, waits for them, and re-layouts  1.67 us (3%)
    pallas_call x1, Pallas kernels, per_device(): pl.pallas_call(gather_kernel, out_shape=jax.ShapeDtypeStruct((1, 128, 512...  50.2 us
    unnamed x1, local copies, waits for them, and re-layouts  1.67 us

profile of v6, /device:TPU:17, one launch (start us, length us, event | category | flops | bytes accessed | tf_op | source)
XLA Modules:
  0.0 51.9 jit_solution(14719365074483688829)
XLA Ops:
  0.0 50.2 %shard_map.37 = f32[1,128,512]{2,1,0:T(8,128)} custom-call(f32[32,64,512]{2,1,0:T(8,128)} %tiles.1, s32[8,32]{1,0:T(8,128)} %bitcast.2, s32[1,32]{1,0:T(1,128)} %bitcast.3), custom_call_target="tpu_custom_call" | custom-call | tf_op jit(solution)/shard_map/pallas_call | solution.py:244
  50.3 1.7 %copy.5 = f32[1,128,512]{2,1,0:T(8,128)} copy(f32[1,128,512]{2,1,0:T(8,128)} %shard_map.37) | data formatting | bytes 524288

commit v7 on v6

--- a/solution.py
+++ b/solution.py
@@ -113,10 +113,13 @@
 
     acc[...] = jnp.zeros_like(acc)
     gram[...] = jnp.zeros_like(gram)
-    for b in range(1, 4):
-        loads[b].wait()
 
     def step_fn(i, carry):
+        @pl.when(i == LAG)
+        def _():
+            for b in range(1, 4):
+                loads[b].wait()
+
         @pl.when(jnp.logical_and(i < CHUNKS, y > 0))
         def _():
             copy_of(mine, i, 0, up).wait_recv()

time: 52.1 us -> 52.1 us (level)
  no operation moved by 1% of the time
where the time goes in v7:
time: 52.1 us; the launch traced here: 52 us
  Pallas kernels  50.3 us (97%)
  local copies, waits for them, and re-layouts  1.67 us (3%)
    pallas_call x1, Pallas kernels, per_device(): pl.pallas_call(gather_kernel, out_shape=jax.ShapeDtypeStruct((1, 128, 512...  50.3 us
    unnamed x1, local copies, waits for them, and re-layouts  1.67 us

profile of v7, /device:TPU:17, one launch (start us, length us, event | category | flops | bytes accessed | tf_op | source)
XLA Modules:
  0.0 52.0 jit_solution(5043617552027385024)
XLA Ops:
  0.0 50.3 %shard_map.37 = f32[1,128,512]{2,1,0:T(8,128)} custom-call(f32[32,64,512]{2,1,0:T(8,128)} %tiles.1, s32[8,32]{1,0:T(8,128)} %bitcast.2, s32[1,32]{1,0:T(1,128)} %bitcast.3), custom_call_target="tpu_custom_call" | custom-call | tf_op jit(solution)/shard_map/pallas_call | solution.py:247
  50.3 1.7 %copy.5 = f32[1,128,512]{2,1,0:T(8,128)} copy(f32[1,128,512]{2,1,0:T(8,128)} %shard_map.37) | data formatting | bytes 524288
